TPU v7x, 512 devices: a whole 4x8x8 slice. The times are simulated.
512 devices in a mesh: sector: 32 (over z_hi, x, core), dof: 16 (over z_lo, y).
Axes of the slice: x: 4, y: 8, z: 8 (z_hi: 4, z_lo: 2; z = z_hi * 2 + z_lo), core: 2. Of those that a mesh axis runs over, the one named last changes fastest.
Arguments:
- rhs: float32 [32, 4096, 128], P('sector', 'dof')
- diagonal: float32 [32, 4096], P('sector', 'dof'), may hold values from 4 to 8
- coupling: bfloat16 [32, 4096, 2048], P('sector', 'dof'), may hold values from -0.125 to 0.125
- springs: float32 [32, 3072], P('sector', 'dof'), may hold values from 1 to 4
- precond: bfloat16 [4096, 4096], P('dof')
- hub_inverse: bfloat16 [3072, 3072], P('dof')
Outputs:
- solution: float32 [32, 4096, 128], P('sector', 'dof')
- residual: float32 [32, 4096, 128], P('sector', 'dof')
All inputs are finite; a program needn't handle non-finite values.
Results may differ from a plain program's by a relative error of at most 0.0056.
Values may be sent and summed in bfloat16 or wider, within the bound.
A program may use at most 64 MiB of HBM per device.

v0:
```python
import jax
import jax.numpy as jnp
from jax import lax
from jax.sharding import PartitionSpec as P

ITERS = 3


def extended(cells, sides, width):
    for axis, dim in sides:
        count = lax.axis_size(axis)
        head = lax.slice_in_dim(cells, 0, width, axis=dim)
        tail = lax.slice_in_dim(cells, cells.shape[dim] - width, cells.shape[dim], axis=dim)
        cells = jnp.concatenate(
            [
                lax.ppermute(tail, axis, [(i, (i + 1) % count) for i in range(count)]),
                cells,
                lax.ppermute(head, axis, [((i + 1) % count, i) for i in range(count)]),
            ],
            axis=dim,
        )
    return cells


def fold_rows(field, update, start_value):
    return update(start_value, lax.all_gather(field, "dof", axis=0, tiled=True), jnp.int32(0))


def product_with(matrix):

    def update(total, piece, start):
        return jnp.dot(matrix, piece, preferred_element_type=jnp.float32)

    return update


def place_rows(total, piece, start):
    return piece


def body(rhs, diagonal, coupling, springs, precond, hub_inverse):
    residual = rhs[0]
    diag_rows = diagonal[0]
    couple_rows = coupling[0]
    spring_rows = springs[0][:, None]
    rows_dev = residual.shape[0]
    loads = residual.shape[1]
    quarter = rows_dev // 4
    parts = lax.axis_size("dof")
    solution = jnp.zeros_like(residual)
    for step in range(ITERS):
        precon = fold_rows(
            residual.astype(jnp.bfloat16),
            product_with(precond),
            jnp.zeros((rows_dev, loads), jnp.float32),
        )
        precon_low = precon.astype(jnp.bfloat16)
        own_faces = precon_low[: 2 * quarter]
        whole = fold_rows(
            own_faces, place_rows, jnp.zeros((parts * 2 * quarter, loads), jnp.bfloat16)
        )
        beside_all = extended(whole[None], (("sector", 0),), 1)
        prev_side = beside_all[0].reshape(parts, 2, quarter, loads)[:, 1]
        next_side = beside_all[2].reshape(parts, 2, quarter, loads)[:, 0]
        needed = jnp.stack([prev_side, next_side], axis=1).reshape(parts * 2 * quarter, loads)
        couple = jnp.dot(couple_rows, needed, preferred_element_type=jnp.float32)
        attached = precon[: 3 * quarter]
        load = lax.psum(spring_rows * attached, "sector")
        hub = fold_rows(
            load.astype(jnp.bfloat16),
            product_with(hub_inverse),
            jnp.zeros((3 * quarter, loads), jnp.float32),
        )
        hub_term = jnp.concatenate(
            [spring_rows * (attached - hub), jnp.zeros((quarter, loads), jnp.float32)], axis=0
        )
        image = diag_rows[:, None] * precon + couple + hub_term
        upper, lower = lax.psum(
            (jnp.sum(image * residual, axis=0), jnp.sum(image * image, axis=0)), ("sector", "dof")
        )
        alpha = upper / (lower + 1e-06)
        solution = solution + alpha * precon
        residual = residual - alpha * image
    return (solution[None], residual[None])


def solution(mesh):
    placed = (
        P("sector", "dof", None),
        P("sector", "dof"),
        P("sector", "dof", None),
        P("sector", "dof"),
        P("dof", None),
        P("dof", None),
    )
    return jax.shard_map(
        body,
        mesh=mesh,
        in_specs=placed,
        out_specs=(P("sector", "dof", None), P("sector", "dof", None)),
        check_vma=False,
    )
```

profile of v0, /device:TPU:1, one launch (start us, length us, event | category | flops | bytes accessed | tf_op | source)
XLA Modules:
  0.0 1211.0 jit_solution(1387459577958328483)
XLA Ops:
  7.2 0.0 copy-start
  7.2 0.0 all-gather.4.cloned.1.call-start
  7.2 1.7 bitcast_convert_fusion
  8.9 0.0 all-gather.4.cloned.1.call-update
  8.9 0.0 copy-start.1
  9.0 0.0 all-gather.6.cloned.1.call-start
  9.0 68.9 %all-gather.4.cloned.1.call-done = bf16[4096,128]{1,0:T(8,128)(2,1)} async-done(((bf16[256,128]{1,0:T(8,128)(2,1)}), bf16[4096,128]{1,0:T(8,128)(2,1)}) %all-gather.4.cloned.1.call-update) | async-done | bytes 1048592 | tf_op jit(solution)/shard_map/all_gather | solution.py:26
  77.9 1.9 fusion.18
  79.8 30.4 %all_gather.28 = bf16[2048,128]{1,0:T(8,128)(2,1)} all-gather(bf16[128,128]{1,0:T(8,128)(2,1)S(1)} %slice.71), channel_id=1, replica_groups=mesh['sector'=32,'dof'=16] {'dof'}, dimensions={0}, use_global_device_ids=true | all-gather | bytes 557056 | tf_op jit(solution)/shard_map/all_gather | solution.py:26
  110.2 19.7 %collective-permute-start.1 = (bf16[1,2048,128]{2,1,0:T(8,128)(2,1)}, bf16[1,2048,128]{2,1,0:T(8,128)(2,1)}, u32[]{:S(2)}, u32[]{:S(2)}) collective-permute-start(bf16[1,2048,128]{2,1,0:T(8,128)(2,1)} %bitcast.2), channel_id=1, source_target_pairs={{16,0},{32,16},{48,32},{64,48},{80,64},{96,80},{112,96},{128,112},... | collective-permute-start | bytes 1572872 | tf_op jit(solution)/shard_map/ppermute | solution.py:18
  129.9 3.0 collective-permute-start
  132.9 0.1 slice_multiply_fusion.2
  133.0 139.5 %psum.63 = bf16[192,128]{1,0:T(8,128)(2,1)} all-reduce(f32[192,128]{1,0:T(8,128)S(1)} %slice_multiply_fusion.2), channel_id=1, replica_groups=mesh['sector'=32,'dof'=16] {'sector'}, use_global_device_ids=true, to_apply=%region_0.0 | all-reduce | flops 24576 | bytes 147456 | tf_op jit(solution)/shard_map/psum | solution.py:68
  272.6 28.3 %all_gather.29 = bf16[3072,128]{1,0:T(8,128)(2,1)S(1)} all-gather(bf16[192,128]{1,0:T(8,128)(2,1)} %psum.63), channel_id=1, replica_groups=mesh['sector'=32,'dof'=16] {'dof'}, dimensions={0}, use_global_device_ids=true | all-gather | bytes 835584 | tf_op jit(solution)/shard_map/all_gather | solution.py:26
  300.8 0.0 copy-start.13
  300.9 0.5 fusion.11
  301.3 0.0 collective-permute-done.1
  301.4 1.0 slice.50
  302.3 0.0 collective-permute-done
  302.3 1.0 slice.49
  303.3 0.1 pad_maximum_fusion
  303.4 1.1 multiply_reduce_fusion.4
  304.5 108.3 %all-reduce.5 = (f32[128]{0:T(128)}, f32[128]{0:T(128)}) all-reduce(f32[128]{0:T(128)S(1)} %get-tuple-element.7, f32[128]{0:T(128)S(1)} %get-tuple-element.6), channel_id=1, replica_groups=mesh['sector'=32,'dof'=16] {'sector','dof'}, use_global_device_ids=true, to_apply=%region_2.0 | all-reduce | flops 256 | bytes 2048 | tf_op jit(solution)/shard_map/psum | solution.py:78
  412.8 0.7 add_divide_fusion.2
  413.5 1.6 fusion.17
  415.1 0.0 all-gather.6.cloned.1.call-update
  415.1 0.0 all-gather.8.cloned.1.call-start
  415.2 56.7 %all-gather.6.cloned.1.call-done = bf16[4096,128]{1,0:T(8,128)(2,1)} async-done(((bf16[256,128]{1,0:T(8,128)(2,1)}), bf16[4096,128]{1,0:T(8,128)(2,1)}) %all-gather.6.cloned.1.call-update) | async-done | bytes 1048592 | tf_op jit(solution)/shard_map/all_gather | solution.py:26
  471.8 1.9 convolution_bitcast_fusion.1
  473.8 0.7 slice_multiply_fusion.1
  474.5 30.4 %all_gather.31 = bf16[2048,128]{1,0:T(8,128)(2,1)} all-gather(bf16[128,128]{1,0:T(8,128)(2,1)S(1)} %slice.70), channel_id=1, replica_groups=mesh['sector'=32,'dof'=16] {'dof'}, dimensions={0}, use_global_device_ids=true | all-gather | bytes 557056 | tf_op jit(solution)/shard_map/all_gather | solution.py:26
  504.9 19.7 %collective-permute-start.3 = (bf16[1,2048,128]{2,1,0:T(8,128)(2,1)}, bf16[1,2048,128]{2,1,0:T(8,128)(2,1)}, u32[]{:S(2)}, u32[]{:S(2)}) collective-permute-start(bf16[1,2048,128]{2,1,0:T(8,128)(2,1)} %bitcast.11), channel_id=1, source_target_pairs={{16,0},{32,16},{48,32},{64,48},{80,64},{96,80},{112,96},{128,112},... | collective-permute-start | bytes 1572872 | tf_op jit(solution)/shard_map/ppermute | solution.py:18
  524.6 3.0 collective-permute-start.2
  527.6 139.7 %psum.66 = bf16[192,128]{1,0:T(8,128)(2,1)} all-reduce(f32[192,128]{1,0:T(8,128)} %slice_multiply_fusion.1), channel_id=1, replica_groups=mesh['sector'=32,'dof'=16] {'sector'}, use_global_device_ids=true, to_apply=%region_5.0 | all-reduce | flops 24576 | bytes 147456 | tf_op jit(solution)/shard_map/psum | solution.py:68
  667.2 28.3 %all_gather.32 = bf16[3072,128]{1,0:T(8,128)(2,1)S(1)} all-gather(bf16[192,128]{1,0:T(8,128)(2,1)} %psum.66), channel_id=1, replica_groups=mesh['sector'=32,'dof'=16] {'dof'}, dimensions={0}, use_global_device_ids=true | all-gather | bytes 835584 | tf_op jit(solution)/shard_map/all_gather | solution.py:26
  695.5 0.5 fusion.9
  696.0 0.0 collective-permute-done.3
  696.0 1.0 slice.54
  697.0 1.0 slice.53
  698.0 0.1 pad_maximum_fusion.1
  698.0 1.7 multiply_reduce_fusion.2
  699.7 108.3 %all-reduce.4 = (f32[128]{0:T(128)}, f32[128]{0:T(128)}) all-reduce(f32[128]{0:T(128)} %get-tuple-element.5, f32[128]{0:T(128)S(1)} %get-tuple-element.4), channel_id=1, replica_groups=mesh['sector'=32,'dof'=16] {'sector','dof'}, use_global_device_ids=true, to_apply=%region_7.0 | all-reduce | flops 256 | bytes 2048 | tf_op jit(solution)/shard_map/psum | solution.py:78
  808.1 0.6 add_divide_fusion.1
  808.7 1.7 fusion.16
  810.3 0.0 all-gather.8.cloned.1.call-update
  810.4 56.7 %all-gather.8.cloned.1.call-done = bf16[4096,128]{1,0:T(8,128)(2,1)} async-done(((bf16[256,128]{1,0:T(8,128)(2,1)}), bf16[4096,128]{1,0:T(8,128)(2,1)}) %all-gather.8.cloned.1.call-update) | async-done | bytes 1048592 | tf_op jit(solution)/shard_map/all_gather | solution.py:26
  867.0 1.9 convolution_bitcast_fusion
  869.0 0.0 copy-start.5
  869.0 0.6 copy-done.5
  869.6 0.7 slice_multiply_fusion
  870.4 30.4 %all_gather.34 = bf16[2048,128]{1,0:T(8,128)(2,1)} all-gather(bf16[128,128]{1,0:T(8,128)(2,1)S(1)} %slice.69), channel_id=1, replica_groups=mesh['sector'=32,'dof'=16] {'dof'}, dimensions={0}, use_global_device_ids=true | all-gather | bytes 557056 | tf_op jit(solution)/shard_map/all_gather | solution.py:26
  900.7 19.7 %collective-permute-start.5 = (bf16[1,2048,128]{2,1,0:T(8,128)(2,1)}, bf16[1,2048,128]{2,1,0:T(8,128)(2,1)}, u32[]{:S(2)}, u32[]{:S(2)}) collective-permute-start(bf16[1,2048,128]{2,1,0:T(8,128)(2,1)} %bitcast.18), channel_id=1, source_target_pairs={{16,0},{32,16},{48,32},{64,48},{80,64},{96,80},{112,96},{128,112},... | collective-permute-start | bytes 1572872 | tf_op jit(solution)/shard_map/ppermute | solution.py:18
  920.4 3.0 collective-permute-start.4
  923.4 139.7 %psum.69 = bf16[192,128]{1,0:T(8,128)(2,1)} all-reduce(f32[192,128]{1,0:T(8,128)} %slice_multiply_fusion), channel_id=1, replica_groups=mesh['sector'=32,'dof'=16] {'sector'}, use_global_device_ids=true, to_apply=%region_10.0 | all-reduce | flops 24576 | bytes 147456 | tf_op jit(solution)/shard_map/psum | solution.py:68
  1063.1 28.3 %all_gather.35 = bf16[3072,128]{1,0:T(8,128)(2,1)S(1)} all-gather(bf16[192,128]{1,0:T(8,128)(2,1)} %psum.69), channel_id=1, replica_groups=mesh['sector'=32,'dof'=16] {'dof'}, dimensions={0}, use_global_device_ids=true | all-gather | bytes 835584 | tf_op jit(solution)/shard_map/all_gather | solution.py:26
  1091.4 1.5 fusion.7
  1092.8 0.0 copy-start.7
  1092.9 0.0 copy-start.10
  1092.9 1.0 slice.58
  1093.9 1.0 slice.57
  1094.9 0.1 pad_maximum_fusion.2
  1095.0 0.5 multiply_reduce_fusion
  1095.4 108.3 %all-reduce.3 = (f32[128]{0:T(128)S(1)}, f32[128]{0:T(128)S(1)}) all-reduce(f32[128]{0:T(128)S(1)} %get-tuple-element.3, f32[128]{0:T(128)S(1)} %get-tuple-element.2), channel_id=1, replica_groups=mesh['sector'=32,'dof'=16] {'sector','dof'}, use_global_device_ids=true, to_apply=%region_12.0 | all-reduce | flops 256 | bytes 2048 | tf_op jit(solution)/shard_map/psum | solution.py:78
  1203.8 0.7 subtract_bitcast_fusion
  (28 shorter events, 0.1 us)
Async XLA Ops:
  7.2 70.7 %copy-start = (bf16[256,4096]{1,0:T(8,128)(2,1)S(1)}, bf16[256,4096]{1,0:T(8,128)(2,1)}, u32[]{:S(2)}) copy-start(bf16[256,4096]{1,0:T(8,128)(2,1)} %param.10) | copy-start | bytes 6291460
  7.2 125.7 %copy-start.12 = (f32[1,192]{1,0:T(1,128)S(1)}, f32[1,192]{1,0:T(1,128)}, u32[]{:S(2)}) copy-start(f32[1,192]{1,0:T(1,128)} %param.9) | copy-start | bytes 2308
  7.2 70.7 %all-gather.4.cloned.1.call-start = ((), (), s32[]{:S(2)}) async-start(), calls=%async_computation | async-start | bytes 1114112 | tf_op jit(solution)/shard_map/all_gather | solution.py:26
  8.9 291.9 %copy-start.1 = (bf16[192,3072]{1,0:T(8,128)(2,1)S(1)}, bf16[192,3072]{1,0:T(8,128)(2,1)}, u32[]{:S(2)}) copy-start(bf16[192,3072]{1,0:T(8,128)(2,1)} %param.11) | copy-start | bytes 3538948
  9.0 462.9 %all-gather.6.cloned.1.call-start = ((), (), s32[]{:S(2)}) async-start(), calls=%async_computation.1 | async-start | bytes 1114112 | tf_op jit(solution)/shard_map/all_gather | solution.py:26
  110.2 191.1 %collective-permute-start.1 = (bf16[1,2048,128]{2,1,0:T(8,128)(2,1)}, bf16[1,2048,128]{2,1,0:T(8,128)(2,1)}, u32[]{:S(2)}, u32[]{:S(2)}) collective-permute-start(bf16[1,2048,128]{2,1,0:T(8,128)(2,1)} %bitcast.2), channel_id=1, source_target_pairs={{16,0},{32,16},{48,32},{64,48},{80,64},{96,80},{112,96},{128,112},... | collective-permute-start | bytes 1572872 | tf_op jit(solution)/shard_map/ppermute | solution.py:18
  129.9 172.4 %collective-permute-start = (bf16[1,2048,128]{2,1,0:T(8,128)(2,1)}, bf16[1,2048,128]{2,1,0:T(8,128)(2,1)}, u32[]{:S(2)}, u32[]{:S(2)}) collective-permute-start(bf16[1,2048,128]{2,1,0:T(8,128)(2,1)} %bitcast.2), channel_id=1, source_target_pairs={{0,16},{16,32},{32,48},{48,64},{64,80},{80,96},{96,112},{112,128},... | collective-permute-start | bytes 1572872 | tf_op jit(solution)/shard_map/ppermute | solution.py:16
  300.8 2.5 copy-start.2
  300.8 2.6 copy-start.8
  300.8 2.6 copy-start.13
  415.1 451.9 %all-gather.8.cloned.1.call-start = ((), (), s32[]{:S(2)}) async-start(), calls=%async_computation.2 | async-start | bytes 1114112 | tf_op jit(solution)/shard_map/all_gather | solution.py:26
  504.9 191.1 %collective-permute-start.3 = (bf16[1,2048,128]{2,1,0:T(8,128)(2,1)}, bf16[1,2048,128]{2,1,0:T(8,128)(2,1)}, u32[]{:S(2)}, u32[]{:S(2)}) collective-permute-start(bf16[1,2048,128]{2,1,0:T(8,128)(2,1)} %bitcast.11), channel_id=1, source_target_pairs={{16,0},{32,16},{48,32},{64,48},{80,64},{96,80},{112,96},{128,112},... | collective-permute-start | bytes 1572872 | tf_op jit(solution)/shard_map/ppermute | solution.py:18
  524.6 172.4 %collective-permute-start.2 = (bf16[1,2048,128]{2,1,0:T(8,128)(2,1)}, bf16[1,2048,128]{2,1,0:T(8,128)(2,1)}, u32[]{:S(2)}, u32[]{:S(2)}) collective-permute-start(bf16[1,2048,128]{2,1,0:T(8,128)(2,1)} %bitcast.11), channel_id=1, source_target_pairs={{0,16},{16,32},{32,48},{48,64},{64,80},{80,96},{96,112},{112,128},... | collective-permute-start | bytes 1572872 | tf_op jit(solution)/shard_map/ppermute | solution.py:16
  695.5 2.5 copy-start.3
  695.5 2.5 copy-start.11
  869.0 0.7 copy-start.5
  900.7 192.1 %collective-permute-start.5 = (bf16[1,2048,128]{2,1,0:T(8,128)(2,1)}, bf16[1,2048,128]{2,1,0:T(8,128)(2,1)}, u32[]{:S(2)}, u32[]{:S(2)}) collective-permute-start(bf16[1,2048,128]{2,1,0:T(8,128)(2,1)} %bitcast.18), channel_id=1, source_target_pairs={{16,0},{32,16},{48,32},{64,48},{80,64},{96,80},{112,96},{128,112},... | collective-permute-start | bytes 1572872 | tf_op jit(solution)/shard_map/ppermute | solution.py:18
  920.4 173.5 %collective-permute-start.4 = (bf16[1,2048,128]{2,1,0:T(8,128)(2,1)}, bf16[1,2048,128]{2,1,0:T(8,128)(2,1)}, u32[]{:S(2)}, u32[]{:S(2)}) collective-permute-start(bf16[1,2048,128]{2,1,0:T(8,128)(2,1)} %bitcast.18), channel_id=1, source_target_pairs={{0,16},{16,32},{32,48},{48,64},{64,80},{80,96},{96,112},{112,128},... | collective-permute-start | bytes 1572872 | tf_op jit(solution)/shard_map/ppermute | solution.py:16
  1091.4 3.6 copy-start.4
  1091.4 3.6 copy-start.6
  1091.4 3.6 copy-start.9
  1092.8 110.9 %copy-start.7 = (f32[256,128]{1,0:T(8,128)S(1)}, f32[256,128]{1,0:T(8,128)}, u32[]{:S(2)}) copy-start(f32[256,128]{1,0:T(8,128)} %copy-done.5) | copy-start | bytes 393220
  1092.9 110.9 %copy-start.10 = (f32[256,128]{1,0:T(8,128)S(1)}, f32[256,128]{1,0:T(8,128)}, u32[]{:S(2)}) copy-start(f32[256,128]{1,0:T(8,128)} %get-tuple-element.15) | copy-start | bytes 393220
Sparse Core Ops, SparseCore 0:
  10.7 67.1 all-gather.3
  415.3 56.5 all-gather.5
  810.5 56.5 all-gather.7
where the time goes:
time: 1210 us
  blocking collectives  920 us (76%)
  waiting for transfers between devices  182 us (15%)
  starting transfers between devices  68.2 us (6%)
  between operations  14.1 us (1%)
    psum x3, blocking collectives, body(): load = lax.psum(spring_rows * attached, 'sector')  419 us
    psum x3, blocking collectives, body(): lax.psum((jnp.sum(image * residual, axis=0), jnp.sum(image * image, axis=...  325 us
    all_gather x3, waiting for transfers between devices, fold_rows(): lax.all_gather(field, 'dof', axis=0, tiled=True)  182 us
    all_gather x6, blocking collectives, fold_rows(): lax.all_gather(field, 'dof', axis=0, tiled=True)  176 us
    ppermute x3, starting transfers between devices, extended(): lax.ppermute(head, axis, [((i + 1) % count, i) for i in range(count)])  59 us
  transfers between devices with their start and end apart: 9, of which 3 were waited for; matrix products, arithmetic and copies ran while one was open for 0% of the time, Pallas kernels for 0%

commit v1 on v0

--- a/solution.py
+++ b/solution.py
@@ -23,7 +23,13 @@
 
 
 def fold_rows(field, update, start_value):
-    return update(start_value, lax.all_gather(field, "dof", axis=0, tiled=True), jnp.int32(0))
+    return update(
+        start_value,
+        jnp.concatenate(
+            lax.all_to_all(jnp.stack([field] * lax.axis_size("dof")), "dof", 0, 0), axis=0
+        ),
+        jnp.int32(0),
+    )
 
 
 def product_with(matrix):

time: 1210 us -> 951 us (0.79)
  waiting for transfers between devices: 182 us -> 11.1 us
  blocking collectives: 920 us -> 830 us
  between operations: 14.1 us -> 1.02 us
    all_gather x3 -> x0, waiting for transfers between devices: 182 us -> none  [fold_rows(): lax.all_gather(field, 'dof', axis=0, tiled=True)]
    all_gather x6 -> x0, blocking collectives: 176 us -> none  [fold_rows(): lax.all_gather(field, 'dof', axis=0, tiled=True)]
    all_to_all x0 -> x3, blocking collectives: none -> 93.7 us  [fold_rows(): lax.all_to_all(jnp.stack([field] * lax.axis_size('dof')), 'dof', 0, 0)]
    all_to_all x0 -> x6, starting transfers between devices: none -> 40.9 us  [fold_rows(): lax.all_to_all(jnp.stack([field] * lax.axis_size('dof')), 'dof', 0, 0)]
    ppermute x3, starting transfers between devices: 59 us -> 26.4 us  [extended(): lax.ppermute(head, axis, [((i + 1) % count, i) for i in range(count)])]
  transfers between devices with their start and end apart: 9 -> 12, of which waited for: 3 -> 6; matrix products, arithmetic and copies ran while one was open for 0% -> 1% of each run, Pallas kernels for 0% -> 0%
where the time goes in v1:
time: 951 us; the launch traced here: 950 us
  blocking collectives  830 us (87%)
  starting transfers between devices  73.1 us (8%)
  local copies, waits for them, and re-layouts  15.4 us (2%)
  waiting for transfers between devices  11.1 us (1%)
  matrix products  10.3 us (1%)
    psum x3, blocking collectives, body(): load = lax.psum(spring_rows * attached, 'sector')  417 us
    psum x3, blocking collectives, body(): lax.psum((jnp.sum(image * residual, axis=0), jnp.sum(image * image, axis=...  320 us
    all_to_all x3, blocking collectives, fold_rows(): lax.all_to_all(jnp.stack([field] * lax.axis_size('dof')), 'dof', 0, 0)  93.7 us
    all_to_all x6, starting transfers between devices, fold_rows(): lax.all_to_all(jnp.stack([field] * lax.axis_size('dof')), 'dof', 0, 0)  40.9 us
    ppermute x3, starting transfers between devices, extended(): lax.ppermute(head, axis, [((i + 1) % count, i) for i in range(count)])  26.4 us
  transfers between devices with their start and end apart: 12, of which 6 were waited for; matrix products, arithmetic and copies ran while one was open for 1% of the time, Pallas kernels for 0%

profile of v1, /device:TPU:1, one launch (start us, length us, event | category | flops | bytes accessed | tf_op | source)
XLA Modules:
  0.0 949.7 jit_solution(3345229381181475859)
XLA Ops:
  0.6 1.1 convert_bitcast_fusion
  1.7 0.2 stack.27
  1.9 34.3 %all_to_all.45 = bf16[16,256,128]{2,1,0:T(8,128)(2,1)S(1)} all-to-all(bf16[16,256,128]{2,1,0:T(8,128)(2,1)S(1)} %stack.27), channel_id=1, replica_groups=mesh['sector'=32,'dof'=16] {'dof'}, dimensions={0} | all-to-all | bytes 2097152 | tf_op jit(solution)/shard_map/all_to_all | solution.py:29
  36.2 0.7 fusion.18
  37.0 0.9 stack.28
  37.9 6.0 all-to-all-start.1
  43.9 0.1 slice_multiply_fusion.2
  44.0 142.7 %psum.63 = bf16[192,128]{1,0:T(8,128)(2,1)} all-reduce(f32[192,128]{1,0:T(8,128)S(1)} %slice_multiply_fusion.2), channel_id=1, replica_groups=mesh['sector'=32,'dof'=16] {'sector'}, use_global_device_ids=true, to_apply=%region_0.0 | all-reduce | flops 24576 | bytes 147456 | tf_op jit(solution)/shard_map/psum | solution.py:74
  186.7 1.8 stack.30
  188.5 7.7 all-to-all-start.2
  196.2 8.8 collective-permute-start.1
  205.0 1.9 collective-permute-start
  206.9 2.7 all-to-all-done.2
  209.6 1.7 fusion.11
  211.3 1.0 slice.50
  212.3 1.0 collective-permute-done
  213.4 1.0 slice.49
  214.3 0.1 pad_maximum_fusion
  214.4 1.1 multiply_reduce_fusion.4
  215.5 106.5 %all-reduce.5 = (f32[128]{0:T(128)}, f32[128]{0:T(128)}) all-reduce(f32[128]{0:T(128)S(1)} %get-tuple-element.7, f32[128]{0:T(128)S(1)} %get-tuple-element.6), channel_id=1, replica_groups=mesh['sector'=32,'dof'=16] {'sector','dof'}, use_global_device_ids=true, to_apply=%region_2.0 | all-reduce | flops 256 | bytes 2048 | tf_op jit(solution)/shard_map/psum | solution.py:84
  322.0 0.7 add_divide_fusion.2
  322.7 1.6 fusion.17
  324.3 0.2 stack.31
  324.5 29.5 %all_to_all.46 = bf16[16,256,128]{2,1,0:T(8,128)(2,1)S(1)} all-to-all(bf16[16,256,128]{2,1,0:T(8,128)(2,1)S(1)} %stack.31), channel_id=1, replica_groups=mesh['sector'=32,'dof'=16] {'dof'}, dimensions={0} | all-to-all | bytes 2097152 | tf_op jit(solution)/shard_map/all_to_all | solution.py:29
  353.9 0.7 convolution_bitcast_fusion.1
  354.7 0.9 stack.32
  355.5 6.4 all-to-all-start.4
  361.9 0.7 slice_multiply_fusion.1
  362.7 137.0 %psum.66 = bf16[192,128]{1,0:T(8,128)(2,1)} all-reduce(f32[192,128]{1,0:T(8,128)} %slice_multiply_fusion.1), channel_id=1, replica_groups=mesh['sector'=32,'dof'=16] {'sector'}, use_global_device_ids=true, to_apply=%region_5.0 | all-reduce | flops 24576 | bytes 147456 | tf_op jit(solution)/shard_map/psum | solution.py:74
  499.7 1.8 stack.34
  501.5 7.2 all-to-all-start.5
  508.7 8.8 collective-permute-start.3
  517.5 1.9 collective-permute-start.2
  519.4 2.7 all-to-all-done.5
  522.1 1.7 fusion.9
  523.8 1.0 slice.54
  524.8 1.1 collective-permute-done.2
  525.9 1.0 slice.53
  526.8 0.1 pad_maximum_fusion.1
  526.9 1.6 multiply_reduce_fusion.2
  528.5 106.5 %all-reduce.4 = (f32[128]{0:T(128)}, f32[128]{0:T(128)}) all-reduce(f32[128]{0:T(128)} %get-tuple-element.5, f32[128]{0:T(128)S(1)} %get-tuple-element.4), channel_id=1, replica_groups=mesh['sector'=32,'dof'=16] {'sector','dof'}, use_global_device_ids=true, to_apply=%region_7.0 | all-reduce | flops 256 | bytes 2048 | tf_op jit(solution)/shard_map/psum | solution.py:84
  635.0 0.7 add_divide_fusion.1
  635.7 1.6 fusion.16
  637.3 0.2 stack.35
  637.5 29.9 %all_to_all.47 = bf16[16,256,128]{2,1,0:T(8,128)(2,1)S(1)} all-to-all(bf16[16,256,128]{2,1,0:T(8,128)(2,1)S(1)} %stack.35), channel_id=1, replica_groups=mesh['sector'=32,'dof'=16] {'dof'}, dimensions={0} | all-to-all | bytes 2097152 | tf_op jit(solution)/shard_map/all_to_all | solution.py:29
  667.4 0.7 convolution_bitcast_fusion
  668.2 0.6 copy-done.5
  668.8 0.9 stack.36
  669.7 6.4 all-to-all-start.7
  676.2 1.6 slice_multiply_fusion
  677.8 136.8 %psum.69 = bf16[192,128]{1,0:T(8,128)(2,1)} all-reduce(f32[192,128]{1,0:T(8,128)} %slice_multiply_fusion), channel_id=1, replica_groups=mesh['sector'=32,'dof'=16] {'sector'}, use_global_device_ids=true, to_apply=%region_10.0 | all-reduce | flops 24576 | bytes 147456 | tf_op jit(solution)/shard_map/psum | solution.py:74
  814.6 1.8 stack.38
  816.5 7.3 all-to-all-start.8
  823.7 8.8 collective-permute-start.5
  832.5 1.9 collective-permute-start.4
  834.4 2.7 all-to-all-done.8
  837.1 1.7 fusion.7
  838.9 1.0 slice.58
  839.9 1.0 collective-permute-done.4
  840.9 1.0 slice.57
  841.8 0.1 pad_maximum_fusion.2
  841.9 0.5 multiply_reduce_fusion
  842.4 106.5 %all-reduce.3 = (f32[128]{0:T(128)S(1)}, f32[128]{0:T(128)S(1)}) all-reduce(f32[128]{0:T(128)S(1)} %get-tuple-element.3, f32[128]{0:T(128)S(1)} %get-tuple-element.2), channel_id=1, replica_groups=mesh['sector'=32,'dof'=16] {'sector','dof'}, use_global_device_ids=true, to_apply=%region_12.0 | all-reduce | flops 256 | bytes 2048 | tf_op jit(solution)/shard_map/psum | solution.py:84
  948.9 0.7 subtract_bitcast_fusion
  (37 shorter events, 0.1 us)
Async XLA Ops:
  0.6 35.6 %copy-start = (bf16[256,4096]{1,0:T(8,128)(2,1)S(1)}, bf16[256,4096]{1,0:T(8,128)(2,1)}, u32[]{:S(2)}) copy-start(bf16[256,4096]{1,0:T(8,128)(2,1)} %param.10) | copy-start | bytes 6291460
  36.2 7.7 copy-start.12
  37.0 172.7 %copy-start.1 = (bf16[192,3072]{1,0:T(8,128)(2,1)S(1)}, bf16[192,3072]{1,0:T(8,128)(2,1)}, u32[]{:S(2)}) copy-start(bf16[192,3072]{1,0:T(8,128)(2,1)} %param.11) | copy-start | bytes 3538948
  37.9 148.8 %all-to-all-start.1 = ((bf16[16,128,128]{2,1,0:T(8,128)(2,1)}), bf16[16,128,128]{2,1,0:T(8,128)(2,1)}, u32[]{:S(2)}, u32[]{:S(2)}) async-start(bf16[16,128,128]{2,1,0:T(8,128)(2,1)} %stack.28), calls=%async_computation.1 | async-start | bytes 1048576 | tf_op jit(solution)/shard_map/all_to_all | solution.py:29
  188.5 21.1 %all-to-all-start.2 = ((bf16[16,192,128]{2,1,0:T(8,128)(2,1)}), bf16[16,192,128]{2,1,0:T(8,128)(2,1)}, u32[]{:S(2)}, u32[]{:S(2)}) async-start(bf16[16,192,128]{2,1,0:T(8,128)(2,1)} %stack.30), calls=%async_computation.2 | async-start | bytes 1572864 | tf_op jit(solution)/shard_map/all_to_all | solution.py:29
  196.2 15.1 %collective-permute-start.1 = (bf16[1,2048,128]{2,1,0:T(8,128)(2,1)}, bf16[1,2048,128]{2,1,0:T(8,128)(2,1)}, u32[]{:S(2)}, u32[]{:S(2)}) collective-permute-start(bf16[1,2048,128]{2,1,0:T(8,128)(2,1)} %bitcast.3), channel_id=1, source_target_pairs={{16,0},{32,16},{48,32},{64,48},{80,64},{96,80},{112,96},{128,112},... | collective-permute-start | bytes 1572872 | tf_op jit(solution)/shard_map/ppermute | solution.py:18
  205.0 8.3 collective-permute-start
  209.6 4.8 copy-start.2
  209.6 4.8 copy-start.8
  209.6 4.8 copy-start.13
  355.5 144.2 %all-to-all-start.4 = ((bf16[16,128,128]{2,1,0:T(8,128)(2,1)}), bf16[16,128,128]{2,1,0:T(8,128)(2,1)}, u32[]{:S(2)}, u32[]{:S(2)}) async-start(bf16[16,128,128]{2,1,0:T(8,128)(2,1)} %stack.32), calls=%async_computation.4 | async-start | bytes 1048576 | tf_op jit(solution)/shard_map/all_to_all | solution.py:29
  501.5 20.6 %all-to-all-start.5 = ((bf16[16,192,128]{2,1,0:T(8,128)(2,1)}), bf16[16,192,128]{2,1,0:T(8,128)(2,1)}, u32[]{:S(2)}, u32[]{:S(2)}) async-start(bf16[16,192,128]{2,1,0:T(8,128)(2,1)} %stack.34), calls=%async_computation.5 | async-start | bytes 1572864 | tf_op jit(solution)/shard_map/all_to_all | solution.py:29
  508.7 15.1 %collective-permute-start.3 = (bf16[1,2048,128]{2,1,0:T(8,128)(2,1)}, bf16[1,2048,128]{2,1,0:T(8,128)(2,1)}, u32[]{:S(2)}, u32[]{:S(2)}) collective-permute-start(bf16[1,2048,128]{2,1,0:T(8,128)(2,1)} %bitcast.15), channel_id=1, source_target_pairs={{16,0},{32,16},{48,32},{64,48},{80,64},{96,80},{112,96},{128,112},... | collective-permute-start | bytes 1572872 | tf_op jit(solution)/shard_map/ppermute | solution.py:18
  517.5 8.3 collective-permute-start.2
  522.1 4.8 copy-start.3
  522.1 4.8 copy-start.11
  668.1 0.7 copy-start.5
  669.7 144.9 %all-to-all-start.7 = ((bf16[16,128,128]{2,1,0:T(8,128)(2,1)}), bf16[16,128,128]{2,1,0:T(8,128)(2,1)}, u32[]{:S(2)}, u32[]{:S(2)}) async-start(bf16[16,128,128]{2,1,0:T(8,128)(2,1)} %stack.36), calls=%async_computation.7 | async-start | bytes 1048576 | tf_op jit(solution)/shard_map/all_to_all | solution.py:29
  816.5 20.7 %all-to-all-start.8 = ((bf16[16,192,128]{2,1,0:T(8,128)(2,1)}), bf16[16,192,128]{2,1,0:T(8,128)(2,1)}, u32[]{:S(2)}, u32[]{:S(2)}) async-start(bf16[16,192,128]{2,1,0:T(8,128)(2,1)} %stack.38), calls=%async_computation.8 | async-start | bytes 1572864 | tf_op jit(solution)/shard_map/all_to_all | solution.py:29
  823.7 15.1 %collective-permute-start.5 = (bf16[1,2048,128]{2,1,0:T(8,128)(2,1)}, bf16[1,2048,128]{2,1,0:T(8,128)(2,1)}, u32[]{:S(2)}, u32[]{:S(2)}) collective-permute-start(bf16[1,2048,128]{2,1,0:T(8,128)(2,1)} %bitcast.24), channel_id=1, source_target_pairs={{16,0},{32,16},{48,32},{64,48},{80,64},{96,80},{112,96},{128,112},... | collective-permute-start | bytes 1572872 | tf_op jit(solution)/shard_map/ppermute | solution.py:18
  832.5 8.3 collective-permute-start.4
  837.1 4.8 copy-start.4
  837.1 4.8 copy-start.6
  837.1 4.8 copy-start.9
  838.8 110.1 %copy-start.7 = (f32[256,128]{1,0:T(8,128)S(1)}, f32[256,128]{1,0:T(8,128)}, u32[]{:S(2)}) copy-start(f32[256,128]{1,0:T(8,128)} %copy-done.5) | copy-start | bytes 393220
  838.8 110.1 %copy-start.10 = (f32[256,128]{1,0:T(8,128)S(1)}, f32[256,128]{1,0:T(8,128)}, u32[]{:S(2)}) copy-start(f32[256,128]{1,0:T(8,128)} %get-tuple-element.15) | copy-start | bytes 393220
